TPU v7x, 256 devices: a whole 4x4x8 slice. The times are simulated.
256 devices in a mesh: ctx: 64 (over y, z, core), head: 4 (over x).
Axes of the slice: x: 4, y: 4, z: 8, core: 2. Of those that a mesh axis runs over, the one named last changes fastest.
Arguments:
- queries: bfloat16 [65536, 4096], P('ctx', 'head'), may hold values from -6.4 to 6.4
- keys: bfloat16 [65536, 4096], P('ctx', 'head'), may hold values from -0.62 to 0.62
- values: bfloat16 [65536, 4096], P('ctx', 'head'), may hold values from -7.6 to 7.6
- log_decay: float32 [32, 65536], P('head', 'ctx'), may hold values from -1.6 to 0, as said below
- gain: float32 [4096], P('head'), may hold values from 0.1 to 1.9
Outputs:
- shift: float32 [4096], P('head')
- covariance: float32 [4096, 2048], P(('head', 'ctx'))
Inputs may be any that keep to these rules, and one draw needn't show every extreme that they name: log_decay is negative everywhere.
All inputs are finite; a program needn't handle non-finite values.
Results may differ from a plain program's by a relative error of at most 0.0045.
The roundings to bfloat16 on the way count: a program that leaves them out, or rounds other values in their place, can miss the bound.
Values may be sent and summed in bfloat16 or wider, within the bound.
A program may use at most 128 MiB of HBM per device.

v0:
```python
import jax
import jax.numpy as jnp
from jax import lax
from jax.sharding import PartitionSpec as P

HEAD_DIM = 128
SPAN = 256


def entering(value, axis, join, neutral):
    count, mine = (lax.axis_size(axis), lax.axis_index(axis))
    pieces = jax.tree.map(lambda part: lax.all_gather(part, axis), value)
    total = jax.tree.map(
        lambda part, zero: jnp.full_like(part, 0) + jnp.asarray(zero, part.dtype), value, neutral
    )

    def turn(position, total):
        longer = join(total, jax.tree.map(lambda part: part[position], pieces))
        return jax.tree.map(lambda new, old: jnp.where(position < mine, new, old), longer, total)

    return lax.fori_loop(0, count - 1, turn, total)


def merged(value, axis, join):
    pieces = jax.tree.map(lambda part: lax.all_gather(part, axis), value)
    head = jax.tree.map(lambda part: part[0], pieces)
    tail = jax.tree.map(lambda part: part[1:], pieces)
    total, _ = lax.scan(lambda total, slab: (join(total, slab), None), head, tail)
    return total


def from_partner(value, axis, apart):
    mask = 2**apart
    pairs = [(source, source ^ mask) for source in range(lax.axis_size(axis))]
    return lax.ppermute(value, axis, pairs)


def block_step(state, inputs):
    query, key, value, decay = inputs
    cumul = jnp.cumsum(decay, axis=1)
    scores = jnp.einsum("thd,shd->hts", query, key, preferred_element_type=jnp.float32)
    length = query.shape[0]
    later = jnp.arange(length)[:, None] >= jnp.arange(length)[None, :]
    diff = cumul[:, :, None] - cumul[:, None, :]
    factor = jnp.where(later[None], jnp.exp(jnp.where(later[None], diff, 0.0)), 0.0)
    weights = (scores * factor).astype(jnp.bfloat16)
    inner = jnp.einsum("hts,shd->thd", weights, value, preferred_element_type=jnp.float32)
    scaled_q = query.astype(jnp.float32) * jnp.exp(cumul).T[:, :, None]
    outer = jnp.einsum("thd,hde->the", scaled_q, state, precision=lax.Precision.HIGHEST)
    scaled_k = key.astype(jnp.float32) * jnp.exp(cumul[:, -1:] - cumul).T[:, :, None]
    update = jnp.einsum(
        "shd,she->hde", scaled_k, value.astype(jnp.float32), precision=lax.Precision.HIGHEST
    )
    new_state = jnp.exp(cumul[:, -1])[:, None, None] * state + update
    return (new_state, inner + outer)


def run_blocks(start, query, key, value, decay):
    count, heads, size = query.shape
    blocks = count // SPAN
    shaped = (
        query.reshape(blocks, SPAN, heads, size),
        key.reshape(blocks, SPAN, heads, size),
        value.reshape(blocks, SPAN, heads, size),
        decay.reshape(heads, blocks, SPAN).transpose(1, 0, 2),
    )
    ending, raw = lax.scan(block_step, start, shaped)
    return (ending, raw.reshape(count, heads, size))


def chain_join(earlier, later):
    return (earlier[0] * later[0], later[0][:, None, None] * earlier[1] + later[1])


def incoming_state(total, ending):
    heads = total.shape[0]
    identity = (jnp.ones((heads,), jnp.float32), jnp.zeros_like(ending))
    carried = entering((total, ending), "ctx", chain_join, identity)
    return carried[1]


def extreme_join(first, second):
    return (jnp.maximum(first[0], second[0]), jnp.minimum(first[1], second[1]))


def body(queries, keys, values, log_decay, gain):
    count, width = queries.shape
    heads = width // HEAD_DIM
    query = queries.reshape(count, heads, HEAD_DIM)
    key = keys.reshape(count, heads, HEAD_DIM)
    value = values.reshape(count, heads, HEAD_DIM)
    cumul = jnp.cumsum(log_decay, axis=1)
    total = jnp.exp(cumul[:, -1])
    scaled_k = key.astype(jnp.float32) * jnp.exp(cumul[:, -1:] - cumul).T[:, :, None]
    ending = jnp.einsum(
        "shd,she->hde", scaled_k, value.astype(jnp.float32), precision=lax.Precision.HIGHEST
    )
    arrived = incoming_state(total, ending)
    _, raw = run_blocks(arrived, query, key, value, log_decay)
    scale = jnp.sqrt(jnp.mean(raw * raw, axis=-1, keepdims=True) + 1e-06)
    attended = (
        (raw / scale * gain.reshape(heads, HEAD_DIM)).reshape(count, width).astype(jnp.bfloat16)
    )
    top, bottom = merged(
        (jnp.max(attended, axis=0), jnp.min(attended, axis=0)), "ctx", extreme_join
    )
    shift = (top.astype(jnp.float32) + bottom.astype(jnp.float32)) / 2.0
    partner = from_partner(attended, "head", 0)
    own_means = jnp.mean(attended.astype(jnp.float32), axis=0)
    other_means = jnp.mean(partner.astype(jnp.float32), axis=0)
    own_centered = (attended.astype(jnp.float32) - own_means).astype(jnp.bfloat16)
    other_centered = (partner.astype(jnp.float32) - other_means).astype(jnp.bfloat16)
    parity = lax.axis_index("head") % 2
    lower = parity == 0
    pair_data = jnp.concatenate(
        [
            jnp.where(lower, own_centered, other_centered),
            jnp.where(lower, other_centered, own_centered),
        ],
        axis=1,
    )
    pair_means = jnp.concatenate(
        [jnp.where(lower, own_means, other_means), jnp.where(lower, other_means, own_means)]
    )
    offset = parity * width
    shards = lax.axis_size("ctx")
    rows = width // shards
    first_row = lax.axis_index("ctx") * rows
    every_mean = lax.all_gather(pair_means[None, :], "ctx", axis=0, tiled=True)
    channel_spread = every_mean - jnp.mean(every_mean, axis=0)
    spread_rows = lax.dynamic_slice_in_dim(channel_spread, offset + first_row, rows, 1)
    fix = count * jnp.dot(spread_rows.T, channel_spread, precision=lax.Precision.HIGHEST)
    gram = lax.psum_scatter(
        lax.dot_general(
            own_centered, pair_data, (((0,), (0,)), ((), ())), preferred_element_type=jnp.float32
        ),
        "ctx",
        scatter_dimension=0,
        tiled=True,
    )
    covariance = (gram + fix) / (count * shards)
    return (shift, covariance)


def solution(mesh):
    placed = (P("ctx", "head"), P("ctx", "head"), P("ctx", "head"), P("head", "ctx"), P("head"))
    return jax.shard_map(
        body,
        mesh=mesh,
        in_specs=placed,
        out_specs=(P("head"), P(("head", "ctx"), None)),
        check_vma=False,
    )
```

profile of v0, /device:TPU:2, one launch (start us, length us, event | category | flops | bytes accessed | tf_op | source)
XLA Modules:
  0.0 510.4 jit_solution(9900833300421825028)
XLA Ops:
  8.0 2.3 reduce-window.14
  10.9 4.1 copy.83
  15.0 6.1 %fusion.24 = f32[8,128,128]{2,1,0:T(8,128)} fusion(f32[1024,8,128]{0,2,1:T(8,128)} %bitcast.142, f32[1024,8]{0,1:T(8,128)S(1)} %exponential_bitcast_fusion.2, bf16[1024,1024]{1,0:T(8,128)(2,1)} %param.13), kind=kOutput, calls=%fused_computation.51 | convolution fusion | flops 1611661312 | bytes 6848512 | tf_op jit(solution)/shard_map/shd,she->hde/dot_general | solution.py:95
  22.7 136.0 %all-reduce = f32[512]{0:T(512)S(1)} all-reduce(f32[512]{0:T(512)S(1)} %bitcast_dynamic-update-slice_fusion), channel_id=2, replica_groups=mesh['ctx'=64,'head'=4] {'ctx'}, use_global_device_ids=true, to_apply=%add | all-reduce | flops 512 | bytes 4096
  158.8 1.9 copy.92
  160.8 1.9 copy.93
  162.7 2.0 copy.94
  164.7 2.1 all-gather.7.cloned.1.call-done
  166.7 76.4 %while.40 = (s32[]{:T(128)}, f32[8,128,128]{2,1,0:T(8,128)S(1)}, s32[]{:T(128)}, f32[64,8]{1,0:T(8,128)S(1)}, f32[64,8,128,128]{3,2,1,0:T(8,128)}, /*index=5*/s32[]{:T(128)}, s32[]{:T(128)}) while((s32[]{:T(128)}, f32[8,128,128]{2,1,0:T(8,128)S(1)}, s32[]{:T(128)}, f32[64,8]{1,0:T(8,128)S(1)}, f32[64,8,128,128]{3,2,1,0:T(8,128)}, ...), condition=%wide.region_3.4_spmd.clone, body=%wide.region_2.3_spmd.clone.sunk | while | flops 524292 | bytes 1573065 | solution.py:21
  168.0 1.2 fusion.45
  169.2 1.2 fusion.45
  172.8 1.2 fusion.45
  174.0 1.2 fusion.45
  175.2 1.2 fusion.45
  178.9 1.2 fusion.45
  180.1 1.2 fusion.45
  243.2 36.9 %while.38 = (s32[]{:T(128)}, f32[8,128,128]{2,1,0:T(8,128)S(1)}, f32[4,256,8,128]{1,3,2,0:T(8,128)}, f32[4,8,256]{2,1,0:T(8,128)}, bf16[4,256,8,128]{3,2,1,0:T(8...) while((s32[]{:T(128)}, f32[8,128,128]{2,1,0:T(8,128)S(1)}, ...), condition=%wide.region_7.8_spmd, body=%wide.region_4.7_spmd.sunk | while | flops 1078265856 | bytes 11248913 | solution.py:67
  244.7 1.3 constant_dynamic-slice_fusion.6
  246.0 1.4 convolution_bitcast_fusion.2
  248.5 2.0 fusion.44
  250.8 1.6 convolution_add_fusion.2
  254.0 1.3 constant_dynamic-slice_fusion.6
  255.2 1.4 convolution_bitcast_fusion.2
  257.7 2.0 fusion.44
  260.0 1.6 convolution_add_fusion.2
  263.2 1.3 constant_dynamic-slice_fusion.6
  264.5 1.4 convolution_bitcast_fusion.2
  267.0 2.0 fusion.44
  269.3 1.6 convolution_add_fusion.2
  272.4 1.3 constant_dynamic-slice_fusion.6
  273.7 1.4 convolution_bitcast_fusion.2
  276.2 2.0 fusion.44
  278.5 1.6 convolution_add_fusion.2
  280.1 2.6 multiply_reduce_fusion
  282.7 5.3 %copy.78 = f32[4,256,8,128]{3,2,1,0:T(8,128)} copy(f32[4,256,8,128]{1,3,2,0:T(8,128)} %get-tuple-element.162) | data formatting | bytes 8388608 | tf_op jit(solution)/shard_map/while | solution.py:67
  290.4 2.2 fusion.19
  293.4 4.2 convert_reduce_fusion.1
  297.6 43.2 %collective-permute-done = bf16[1024,1024]{1,0:T(8,128)(2,1)} collective-permute-done((bf16[1024,1024]{1,0:T(8,128)(2,1)S(1)}, bf16[1024,1024]{1,0:T(8,128)(2,1)}, u32[]{:S(2)}, u32[]{:S(2)}) %collective-permute-start) | collective-permute-done | bytes 2097184 | tf_op jit(solution)/shard_map/ppermute | solution.py:35
  340.7 2.0 convert_reduce_fusion
  342.7 2.8 broadcast_select_fusion.1
  345.5 7.0 %fusion.20 = f32[1024,2048]{1,0:T(8,128)} fusion(bf16[1024,1024]{1,0:T(8,128)(2,1)S(1)} %get-tuple-element.263, bf16[1024,1024]{1,0:T(8,128)(2,1)S(1)} %get-tuple-element.262, bf16[1024,1024]{1,0:T(8,128)(2,1)S(1)} %fusion.19, f32[1024]{0:T(1024)S(1)} %multiply_bitcast_fusion), kind=kOutput, calls=%fused_computation.43 | convolution fusion | flops 4306501632 | bytes 14684160 | tf_op jit(solution)/shard_map/dot_general | solution.py:134
  352.5 1.6 copy-done.3
  354.9 42.3 %all-gather.4 = bf16[64,1,1024]{2,1,0:T(2,128)(2,1)S(1)} all-gather(bf16[1,1,1024]{2,1,0:T(2,128)(2,1)S(1)} %reshape.171), channel_id=1, replica_groups=mesh['ctx'=64,'head'=4] {'ctx'}, dimensions={0}, use_global_device_ids=true | all-gather | bytes 133120 | tf_op jit(solution)/shard_map/all_gather | solution.py:25
  397.5 43.1 %all-gather.3 = bf16[64,1,1024]{2,1,0:T(2,128)(2,1)S(1)} all-gather(bf16[1,1,1024]{2,1,0:T(2,128)(2,1)S(1)} %reshape.169), channel_id=1, replica_groups=mesh['ctx'=64,'head'=4] {'ctx'}, dimensions={0}, use_global_device_ids=true | all-gather | bytes 133120 | tf_op jit(solution)/shard_map/all_gather | solution.py:25
  441.0 5.5 %while.39 = (s32[]{:T(128)}, bf16[1024]{0:T(1024)(128)(2,1)S(1)}, bf16[1024]{0:T(1024)(128)(2,1)S(1)}, bf16[63,1024]{1,0:T(8,128)(2,1)S(1)}, bf16[63,1024]{1,0:T(8,128)(2,1)S(1)}, /*index=5*/s32[]{:T(128)}) while((s32[]{:T(128)}, bf16[1024]{0:T(1024)(128)(2,1)S(1)}, bf16[1024]{0:T(1024)(128)(2,1)S(1)}, bf16[63,1024]{1,0:T(8,128)(2,1)S(1)}, ...), condition=%wide.region_12.13_spmd, body=%wide.region_11.12_spmd.sunk | while | flops 2050 | bytes 20553 | solution.py:28
  447.1 48.6 %all-gather.2 = f32[131072]{0:T(1024)S(1)} all-gather(f32[2048]{0:T(1024)S(1)} %pad_maximum_fusion), channel_id=4, replica_groups=mesh['ctx'=64,'head'=4] {'ctx'}, dimensions={0}, use_global_device_ids=true | all-gather | bytes 532480 | tf_op jit(solution)/shard_map/all_gather | solution.py:129
  496.3 5.7 %reduce-scatter.2.cloned.1.call-done = f32[16,2048]{1,0:T(8,128)} async-done(((f32[1024,2048]{1,0:T(8,128)}), f32[16,2048]{1,0:T(8,128)}) %reduce-scatter.2.cloned.1.call-update) | async-done | bytes 131088 | tf_op jit(solution)/shard_map/reduce_scatter | solution.py:133
  502.0 1.6 add_multiply_fusion
  (405 shorter events, 90.7 us)
Async XLA Ops:
  7.2 159.6 %all-gather.7.cloned.1.call-start = ((), (), s32[]{:S(2)}) async-start(), calls=%async_computation.2 | async-start | bytes 34078720 | tf_op jit(solution)/shard_map/all_gather | solution.py:12
  15.0 6.3 %copy-start.6 = (u32[256]{0:T(256)S(1)}, u32[256]{0:T(256)}, u32[]{:S(2)}) copy-start(u32[256]{0:T(256)} %constant.110) | copy-start | bytes 3076
  15.0 143.8 %copy-start.1 = (bf16[1024,1024]{1,0:T(8,128)(2,1)S(1)}, bf16[1024,1024]{1,0:T(8,128)(2,1)}, u32[]{:S(2)}) copy-start(bf16[1024,1024]{1,0:T(8,128)(2,1)} %param.12) | copy-start | bytes 6291460
  21.2 480.8 %reduce-scatter.2.cloned.1.call-start = ((), (), s32[]{:S(2)}) async-start(), calls=%async_computation.1 | async-start | bytes 8519680 | tf_op jit(solution)/shard_map/reduce_scatter | solution.py:133
  158.8 2.0 copy-start.2
  158.8 3.9 copy-start.4
  287.9 1.4 copy-start.5
  288.2 2.2 copy-start
  292.5 48.2 %collective-permute-start = (bf16[1024,1024]{1,0:T(8,128)(2,1)S(1)}, bf16[1024,1024]{1,0:T(8,128)(2,1)}, u32[]{:S(2)}, u32[]{:S(2)}) collective-permute-start(bf16[1024,1024]{1,0:T(8,128)(2,1)S(1)} %fusion.19), channel_id=1, source_target_pairs={{0,1},{1,0},{2,3},{3,2},{4,5},{5,4},{6,7},{7,6},{8,9},{9,8},{10,11... | collective-permute-start | bytes 6291464 | tf_op jit(solution)/shard_map/ppermute | solution.py:35
  352.5 1.6 copy-start.3
Sparse Core Ops, SparseCore 0:
  21.3 145.3 all-gather.6
  352.6 149.3 reduce-scatter.1
where the time goes:
time: 514 us; the launch traced here: 510 us
  blocking collectives  270 us (53%)
  other arithmetic  98.1 us (19%)
  waiting for transfers between devices  51 us (10%)
  local copies, waits for them, and re-layouts  38.8 us (8%)
  matrix products  33.5 us (7%)
  between operations  14.9 us (3%)
    unnamed x1, blocking collectives  136 us
    all_gather x2, blocking collectives, merged(): pieces = jax.tree.map(lambda part: lax.all_gather(part, axis), value)  85.3 us
    select_n x63, other arithmetic, turn(): jnp.where(position < mine, new, old)  73.9 us
    all_gather x1, blocking collectives, body(): every_mean = lax.all_gather(pair_means[None, :], 'ctx', axis=0, tiled=True)  48.6 us
    ppermute x1, waiting for transfers between devices, from_partner(): return lax.ppermute(value, axis, pairs)  43.2 us
  transfers between devices with their start and end apart: 3, of which 3 were waited for; matrix products, arithmetic and copies ran while one was open for 4% of the time, Pallas kernels for 0%

commit v1 on v0

--- a/solution.py
+++ b/solution.py
@@ -1,3 +1,4 @@
+import functools
 import jax
 import jax.numpy as jnp
 from jax import lax
@@ -5,6 +6,15 @@
 
 HEAD_DIM = 128
 SPAN = 256
+
+
+def lift_lots_all(x0, mesh_ax, dim_at):
+    outcome_arr = jnp.stack([x0] * jax.lax.axis_size(mesh_ax))
+    far_arr = jax.lax.all_to_all(outcome_arr, axis_name=mesh_ax, split_axis=0, concat_axis=0)
+    return jnp.concatenate(far_arr, axis=dim_at)
+
+
+groups_choose = functools.partial(lift_lots_all, mesh_ax="ctx", dim_at=0)
 
 
 def entering(value, axis, join, neutral):
@@ -126,7 +136,7 @@
     shards = lax.axis_size("ctx")
     rows = width // shards
     first_row = lax.axis_index("ctx") * rows
-    every_mean = lax.all_gather(pair_means[None, :], "ctx", axis=0, tiled=True)
+    every_mean = groups_choose(pair_means[None, :])
     channel_spread = every_mean - jnp.mean(every_mean, axis=0)
     spread_rows = lax.dynamic_slice_in_dim(channel_spread, offset + first_row, rows, 1)
     fix = count * jnp.dot(spread_rows.T, channel_spread, precision=lax.Precision.HIGHEST)

time: 514 us -> 514 us (level)
  blocking collectives: 270 us -> 229 us
  waiting for transfers between devices: 51 us -> 86 us
  starting transfers between devices: 0.95 us -> 6.96 us
    all_gather x1 -> x0, blocking collectives: 48.6 us -> none  [body(): every_mean = lax.all_gather(pair_means[None, :], 'ctx', axis=0, tiled=True)]
    reduce_scatter x1, waiting for transfers between devices: 5.7 us -> 40.8 us  [body(): lax.psum_scatter(lax.dot_general(own_centered, pair_data, (((0,), (0,)),...]
    all_gather x2, blocking collectives: 85.3 us -> 92.8 us  [merged(): pieces = jax.tree.map(lambda part: lax.all_gather(part, axis), value)]
    all_to_all x0 -> x1, starting transfers between devices: none -> 6.01 us  [lift_lots_all(): jax.lax.all_to_all(outcome_arr, axis_name=mesh_ax, split_axis=0, concat_a...]
  transfers between devices with their start and end apart: 3 -> 4, of which waited for: 3 -> 3; matrix products, arithmetic and copies ran while one was open for 4% -> 4% of each run, Pallas kernels for 0% -> 0%
where the time goes in v1:
time: 514 us; the launch traced here: 510 us
  blocking collectives  229 us (45%)
  other arithmetic  98.5 us (19%)
  waiting for transfers between devices  86 us (17%)
  local copies, waits for them, and re-layouts  38.2 us (7%)
  matrix products  33.5 us (7%)
  between operations  14.9 us (3%)
  starting transfers between devices  6.96 us (1%)
    unnamed x1, blocking collectives  136 us
    all_gather x2, blocking collectives, merged(): pieces = jax.tree.map(lambda part: lax.all_gather(part, axis), value)  92.8 us
    select_n x63, other arithmetic, turn(): jnp.where(position < mine, new, old)  73.9 us
    ppermute x1, waiting for transfers between devices, from_partner(): return lax.ppermute(value, axis, pairs)  43.2 us
    reduce_scatter x1, waiting for transfers between devices, body(): lax.psum_scatter(lax.dot_general(own_centered, pair_data, (((0,), (0,)),...  40.8 us
  transfers between devices with their start and end apart: 4, of which 3 were waited for; matrix products, arithmetic and copies ran while one was open for 4% of the time, Pallas kernels for 0%

profile of v1, /device:TPU:2, one launch (start us, length us, event | category | flops | bytes accessed | tf_op | source)
XLA Modules:
  0.0 510.3 jit_solution(13979369654597585410)
XLA Ops:
  8.0 2.3 reduce-window.14
  10.9 4.1 copy.98
  15.0 6.1 %fusion.24 = f32[8,128,128]{2,1,0:T(8,128)} fusion(f32[1024,8,128]{0,2,1:T(8,128)} %bitcast.144, f32[1024,8]{0,1:T(8,128)S(1)} %exponential_bitcast_fusion.2, bf16[1024,1024]{1,0:T(8,128)(2,1)} %param.13), kind=kOutput, calls=%fused_computation.51 | convolution fusion | flops 1611661312 | bytes 6848512 | tf_op jit(solution)/shard_map/shd,she->hde/dot_general | solution.py:105
  22.7 136.0 %all-reduce = f32[512]{0:T(512)S(1)} all-reduce(f32[512]{0:T(512)S(1)} %bitcast_dynamic-update-slice_fusion), channel_id=2, replica_groups=mesh['ctx'=64,'head'=4] {'ctx'}, use_global_device_ids=true, to_apply=%add | all-reduce | flops 512 | bytes 4096
  158.8 1.9 copy.109
  160.8 1.9 copy.110
  162.7 2.0 copy.111
  164.7 2.1 all-gather.6.cloned.1.call-done
  166.7 76.4 %while.40 = (s32[]{:T(128)}, f32[8,128,128]{2,1,0:T(8,128)S(1)}, s32[]{:T(128)}, f32[64,8]{1,0:T(8,128)S(1)}, f32[64,8,128,128]{3,2,1,0:T(8,128)}, /*index=5*/s32[]{:T(128)}, s32[]{:T(128)}) while((s32[]{:T(128)}, f32[8,128,128]{2,1,0:T(8,128)S(1)}, s32[]{:T(128)}, f32[64,8]{1,0:T(8,128)S(1)}, f32[64,8,128,128]{3,2,1,0:T(8,128)}, ...), condition=%wide.region_3.4_spmd.clone, body=%wide.region_2.3_spmd.clone.sunk | while | flops 524292 | bytes 1573065 | solution.py:31
  168.0 1.2 fusion.45
  169.2 1.2 fusion.45
  172.8 1.2 fusion.45
  174.0 1.2 fusion.45
  175.2 1.2 fusion.45
  178.9 1.2 fusion.45
  180.1 1.2 fusion.45
  183.7 1.2 fusion.45
  243.2 36.9 %while.38 = (s32[]{:T(128)}, f32[8,128,128]{2,1,0:T(8,128)S(1)}, f32[4,256,8,128]{1,3,2,0:T(8,128)}, f32[4,8,256]{2,1,0:T(8,128)}, bf16[4,256,8,128]{3,2,1,0:T(8...) while((s32[]{:T(128)}, f32[8,128,128]{2,1,0:T(8,128)S(1)}, ...), condition=%wide.region_7.8_spmd, body=%wide.region_4.7_spmd.sunk | while | flops 1078265856 | bytes 11248913 | solution.py:77
  244.7 1.3 constant_dynamic-slice_fusion.6
  246.0 1.4 convolution_bitcast_fusion.2
  248.5 2.0 fusion.44
  250.8 1.6 convolution_add_fusion.2
  254.0 1.3 constant_dynamic-slice_fusion.6
  255.2 1.4 convolution_bitcast_fusion.2
  257.7 2.0 fusion.44
  260.0 1.6 convolution_add_fusion.2
  263.2 1.3 constant_dynamic-slice_fusion.6
  264.5 1.4 convolution_bitcast_fusion.2
  267.0 2.0 fusion.44
  269.3 1.6 convolution_add_fusion.2
  272.4 1.3 constant_dynamic-slice_fusion.6
  273.7 1.4 convolution_bitcast_fusion.2
  276.2 2.0 fusion.44
  278.5 1.6 convolution_add_fusion.2
  280.1 2.6 multiply_reduce_fusion
  282.7 5.3 %copy.92 = f32[4,256,8,128]{3,2,1,0:T(8,128)} copy(f32[4,256,8,128]{1,3,2,0:T(8,128)} %get-tuple-element.162) | data formatting | bytes 8388608 | tf_op jit(solution)/shard_map/while | solution.py:77
  290.4 2.2 fusion.19
  293.4 4.2 convert_reduce_fusion.1
  297.6 43.2 %collective-permute-done = bf16[1024,1024]{1,0:T(8,128)(2,1)} collective-permute-done((bf16[1024,1024]{1,0:T(8,128)(2,1)S(1)}, bf16[1024,1024]{1,0:T(8,128)(2,1)}, u32[]{:S(2)}, u32[]{:S(2)}) %collective-permute-start) | collective-permute-done | bytes 2097184 | tf_op jit(solution)/shard_map/ppermute | solution.py:45
  340.7 2.0 convert_reduce_fusion
  342.7 2.8 broadcast_select_fusion.1
  345.5 7.0 %fusion.20 = f32[1024,2048]{1,0:T(8,128)} fusion(bf16[1024,1024]{1,0:T(8,128)(2,1)S(1)} %get-tuple-element.270, bf16[1024,1024]{1,0:T(8,128)(2,1)S(1)} %get-tuple-element.269, bf16[1024,1024]{1,0:T(8,128)(2,1)S(1)} %fusion.19, f32[1024]{0:T(1024)S(1)} %multiply_bitcast_fusion), kind=kOutput, calls=%fused_computation.43 | convolution fusion | flops 4306501632 | bytes 14684160 | tf_op jit(solution)/shard_map/dot_general | solution.py:144
  353.6 6.0 %all-to-all-start = ((f32[64,1,2048]{2,1,0:T(1,128)}), f32[64,1,2048]{2,1,0:T(1,128)S(1)}, u32[]{:S(2)}, u32[]{:S(2)}) async-start(f32[64,1,2048]{2,1,0:T(1,128)} %stack.3), calls=%async_computation.1 | async-start | bytes 1048576 | tf_op jit(solution)/shard_map/all_to_all | solution.py:13
  360.5 49.1 %all-gather.3 = bf16[64,1,1024]{2,1,0:T(2,128)(2,1)S(1)} all-gather(bf16[1,1,1024]{2,1,0:T(2,128)(2,1)S(1)} %reshape.176), channel_id=1, replica_groups=mesh['ctx'=64,'head'=4] {'ctx'}, dimensions={0}, use_global_device_ids=true | all-gather | bytes 133120 | tf_op jit(solution)/shard_map/all_gather | solution.py:35
  410.0 43.7 %all-gather.2 = bf16[64,1,1024]{2,1,0:T(2,128)(2,1)S(1)} all-gather(bf16[1,1,1024]{2,1,0:T(2,128)(2,1)S(1)} %reshape.174), channel_id=1, replica_groups=mesh['ctx'=64,'head'=4] {'ctx'}, dimensions={0}, use_global_device_ids=true | all-gather | bytes 133120 | tf_op jit(solution)/shard_map/all_gather | solution.py:35
  454.1 5.5 %while.39 = (s32[]{:T(128)}, bf16[1024]{0:T(1024)(128)(2,1)S(1)}, bf16[1024]{0:T(1024)(128)(2,1)S(1)}, bf16[63,1024]{1,0:T(8,128)(2,1)S(1)}, bf16[63,1024]{1,0:T(8,128)(2,1)S(1)}, /*index=5*/s32[]{:T(128)}) while((s32[]{:T(128)}, bf16[1024]{0:T(1024)(128)(2,1)S(1)}, bf16[1024]{0:T(1024)(128)(2,1)S(1)}, bf16[63,1024]{1,0:T(8,128)(2,1)S(1)}, ...), condition=%wide.region_12.13_spmd, body=%wide.region_11.12_spmd.sunk | while | flops 2050 | bytes 20553 | solution.py:38
  461.1 40.8 %reduce-scatter.2.cloned.1.call-done = f32[16,2048]{1,0:T(8,128)} async-done(((f32[1024,2048]{1,0:T(8,128)}), f32[16,2048]{1,0:T(8,128)}) %reduce-scatter.2.cloned.1.call-update) | async-done | bytes 131088 | tf_op jit(solution)/shard_map/reduce_scatter | solution.py:143
  501.9 1.6 add_multiply_fusion
  (406 shorter events, 91.0 us)
Async XLA Ops:
  7.2 159.6 %all-gather.6.cloned.1.call-start = ((), (), s32[]{:S(2)}) async-start(), calls=%async_computation.3 | async-start | bytes 34078720 | tf_op jit(solution)/shard_map/all_gather | solution.py:22
  15.0 6.3 %copy-start.6 = (u32[256]{0:T(256)S(1)}, u32[256]{0:T(256)}, u32[]{:S(2)}) copy-start(u32[256]{0:T(256)} %constant.110) | copy-start | bytes 3076
  15.0 143.8 %copy-start.1 = (bf16[1024,1024]{1,0:T(8,128)(2,1)S(1)}, bf16[1024,1024]{1,0:T(8,128)(2,1)}, u32[]{:S(2)}) copy-start(bf16[1024,1024]{1,0:T(8,128)(2,1)} %param.12) | copy-start | bytes 6291460
  21.2 480.7 %reduce-scatter.2.cloned.1.call-start = ((), (), s32[]{:S(2)}) async-start(), calls=%async_computation.2 | async-start | bytes 8519680 | tf_op jit(solution)/shard_map/reduce_scatter | solution.py:143
  158.8 2.0 copy-start.2
  158.8 3.9 copy-start.4
  287.9 1.4 copy-start.5
  288.2 2.2 copy-start
  292.5 48.2 %collective-permute-start = (bf16[1024,1024]{1,0:T(8,128)(2,1)S(1)}, bf16[1024,1024]{1,0:T(8,128)(2,1)}, u32[]{:S(2)}, u32[]{:S(2)}) collective-permute-start(bf16[1024,1024]{1,0:T(8,128)(2,1)S(1)} %fusion.19), channel_id=1, source_target_pairs={{0,1},{1,0},{2,3},{3,2},{4,5},{5,4},{6,7},{7,6},{8,9},{9,8},{10,11... | collective-permute-start | bytes 6291464 | tf_op jit(solution)/shard_map/ppermute | solution.py:45
  352.5 7.2 %copy-start.3 = (bf16[4,256,8,128]{1,3,2,0:T(8,128)(2,1)S(1)}, bf16[4,256,8,128]{1,3,2,0:T(8,128)(2,1)}, u32[]{:S(2)}) copy-start(bf16[4,256,8,128]{1,3,2,0:T(8,128)(2,1)} %get-tuple-element.264) | copy-start | bytes 6291460
  353.6 106.6 %all-to-all-start = ((f32[64,1,2048]{2,1,0:T(1,128)}), f32[64,1,2048]{2,1,0:T(1,128)S(1)}, u32[]{:S(2)}, u32[]{:S(2)}) async-start(f32[64,1,2048]{2,1,0:T(1,128)} %stack.3), calls=%async_computation.1 | async-start | bytes 1048576 | tf_op jit(solution)/shard_map/all_to_all | solution.py:13
Sparse Core Ops, SparseCore 0:
  21.3 145.3 all-gather.5
  352.6 149.2 reduce-scatter.1
